TPU v7x, 256 devices: a whole 4x4x8 slice. The times are simulated.
256 devices in a mesh: modes: 8 (over z_hi, x), space: 32 (over z_lo, y, core).
Axes of the slice: x: 4, y: 4, z: 8 (z_hi: 2, z_lo: 4; z = z_hi * 4 + z_lo), core: 2. Of those that a mesh axis runs over, the one named last changes fastest.
Arguments:
- mode_coeffs: float32 [120, 32, 120, 128], P('modes', 'space'), may hold values from -6 to 6
- mean_perm: float32 [32, 120, 128], P('space'), may hold values from 0.5 to 2
- kl_fields: float32 [7, 32, 120, 128], P(None, 'space'), may hold values from -4 to 4
- couplings: float32 [7, 120, 120], replicated, may hold values from -0.5 to 0.5
Outputs:
- applied: float32 [120, 32, 120, 128], P('modes', 'space')
All inputs are finite; a program needn't handle non-finite values.
Results may differ from a plain program's by a relative error of at most 0.0001.
Values sent between devices are 32-bit elements; how exact they have to be, the bound alone decides.
A program may use at most 192 MiB of HBM per device.

v0:
```python
import jax
import jax.numpy as jnp
from jax import lax
from jax.sharding import PartitionSpec as P


def extended(block, sides, width):
    for axis, dim in sides:
        count = lax.axis_size(axis)
        forward = [(i, i + 1) for i in range(count - 1)]
        backward = [(target, source) for source, target in forward]
        low = lax.ppermute(
            lax.slice_in_dim(block, block.shape[dim] - width, None, axis=dim), axis, forward
        )
        high = lax.ppermute(lax.slice_in_dim(block, 0, width, axis=dim), axis, backward)
        block = jnp.concatenate([low, block, high], axis=dim)
    return block


def shifted(padded, direction, offset):
    result = padded
    base = padded.ndim - 3
    for axis_index in range(3):
        extent = padded.shape[base + axis_index] - 2
        begin = offset if axis_index == direction else 1
        result = lax.slice_in_dim(result, begin, begin + extent, axis=base + axis_index)
    return result


def operate(field_pad, perm_pad):
    centre = shifted(field_pad, 0, 1)
    centre_perm = shifted(perm_pad, 0, 1)
    terms = []
    for direction in range(3):
        for offset in (0, 2):
            face_perm = 0.5 * (centre_perm + shifted(perm_pad, direction, offset))
            terms.append(face_perm * (centre - shifted(field_pad, direction, offset)))
    accum_total = terms[0]
    for extra_term in terms[1:]:
        accum_total = accum_total + extra_term
    return accum_total


def local(mode_coeffs, mean_perm, kl_fields, couplings):
    mode_dev = mode_coeffs.shape[0]
    shape_cells = mode_coeffs.shape[1:]
    term_count = kl_fields.shape[0] + 1
    all_perm = jnp.concatenate([mean_perm[None], kl_fields], 0)
    perm_halo = extended(all_perm, (("space", 1),), 1)
    perm_pad = jnp.pad(perm_halo, ((0, 0), (0, 0), (1, 1), (1, 1)))[:, None]
    first_mode = lax.axis_index("modes") * mode_dev
    own_rows = lax.dynamic_slice_in_dim(couplings, first_mode, mode_dev, 1)
    block_piece = lax.all_gather(mode_coeffs, "modes", axis=0, tiled=True)
    flat_piece = block_piece.reshape(block_piece.shape[0], -1)
    mixed_modes = jnp.einsum("kin,nc->kic", own_rows, flat_piece, precision=lax.Precision.HIGHEST)
    fields = jnp.concatenate(
        [mode_coeffs[None], mixed_modes.reshape((term_count - 1, mode_dev) + shape_cells)], 0
    )
    field_halo = extended(fields, (("space", 2),), 1)
    field_pad = jnp.pad(field_halo, ((0, 0), (0, 0), (0, 0), (1, 1), (1, 1)))
    return jnp.sum(operate(field_pad, perm_pad), axis=0)


def solution(mesh):
    in_specs = (
        P("modes", "space", None, None),
        P("space", None, None),
        P(None, "space", None, None),
        P(),
    )
    out_specs = P("modes", "space", None, None)
    return jax.shard_map(local, mesh=mesh, in_specs=in_specs, out_specs=out_specs, check_vma=False)
```

profile of v0, /device:TPU:1, one launch (start us, length us, event | category | flops | bytes accessed | tf_op | source)
XLA Modules:
  0.0 360.3 jit_solution(1196285301615844768)
XLA Ops:
  6.5 0.0 copy-start
  6.5 0.0 all-gather.2.cloned.1.call-start
  6.5 0.7 all-gather.2.cloned.1.call-update
  7.3 1.4 copy.32
  8.6 161.9 %all-gather.2.cloned.1.call-done = f32[120,1,120,128]{3,2,1,0:T(8,128)} async-done(((f32[15,1,120,128]{3,2,1,0:T(8,128)}), f32[120,1,120,128]{3,2,1,0:T(8,128)}) %all-gather.2.cloned.1.call-update) | async-done | bytes 7372816 | tf_op jit(solution)/shard_map/all_gather | solution.py:53
  170.5 0.0 copy-done
  170.5 10.9 %fusion.18 = f32[7,15,1,120,128]{4,1,3,0,2:T(8,128)S(1)} fusion(f32[7,120,120]{2,1,0:T(8,128)S(1)} %copy-done, s32[]{:T(128)S(6)} %select_n.3, f32[15,8,120,128]{3,2,1,0:T(8,128)} %bitcast.50), kind=kOutput, calls=%fused_computation.39 | convolution fusion | flops 2322432000 | bytes 13881348 | tf_op jit(solution)/shard_map/kin,nc->kic/dot_general | solution.py:55
  181.4 0.6 pad_maximum_fusion
  182.0 0.0 copy-start.3
  182.0 0.0 copy-start.4
  182.0 5.2 %copy.10 = f32[8,15,1,120,128]{4,3,2,1,0:T(8,128)} copy(f32[8,15,1,120,128]{4,1,3,0,2:T(8,128)S(1)} %pad_maximum_fusion) | data formatting | bytes 14745600 | tf_op jit(solution)/shard_map/concatenate | solution.py:56
  187.2 4.1 %collective-permute-start.2 = (f32[8,15,1,120,128]{4,3,2,1,0:T(8,128)}, f32[8,15,1,120,128]{4,3,2,1,0:T(8,128)S(1)}, u32[]{:S(2)}, u32[]{:S(2)}) collective-permute-start(f32[8,15,1,120,128]{4,3,2,1,0:T(8,128)} %copy.10), channel_id=1, source_target_pairs={{0,1},{1,2},{2,3},{3,4},{4,5},{5,6},{6,7},{7,8},{8,9},{9,10},{10,1... | collective-permute-start | bytes 22118408 | tf_op jit(solution)/shard_map/ppermute | solution.py:12
  191.3 1.9 collective-permute-start.3
  193.2 0.0 copy-done.3
  193.2 0.0 copy-done.4
  193.3 3.6 %collective-permute-start = (f32[8,1,120,128]{3,2,1,0:T(8,128)S(1)}, f32[8,1,120,128]{3,2,1,0:T(8,128)S(1)}, u32[]{:S(2)}, u32[]{:S(2)}) collective-permute-start(f32[8,1,120,128]{3,2,1,0:T(8,128)S(1)} %pad_maximum_fusion.1), channel_id=1, source_target_pairs={{0,1},{1,2},{2,3},{3,4},{4,5},{5,6},{6,7},{7,8},{8,9},{9,10},{10,1... | collective-permute-start | bytes 1474568 | tf_op jit(solution)/shard_map/ppermute | solution.py:12
  196.9 2.1 collective-permute-start.1
  199.0 77.2 %collective-permute-done = f32[8,1,120,128]{3,2,1,0:T(8,128)S(1)} collective-permute-done((f32[8,1,120,128]{3,2,1,0:T(8,128)S(1)}, f32[8,1,120,128]{3,2,1,0:T(8,128)S(1)}, u32[]{:S(2)}, u32[]{:S(2)}) %collective-permute-start) | collective-permute-done | bytes 491552 | tf_op jit(solution)/shard_map/ppermute | solution.py:12
  276.2 4.4 %collective-permute-done.1 = f32[8,1,120,128]{3,2,1,0:T(8,128)S(1)} collective-permute-done((f32[8,1,120,128]{3,2,1,0:T(8,128)S(1)}, f32[8,1,120,128]{3,2,1,0:T(8,128)S(1)}, u32[]{:S(2)}, u32[]{:S(2)}) %collective-permute-start.1) | collective-permute-done | bytes 491552 | tf_op jit(solution)/shard_map/ppermute | solution.py:15
  280.6 1.6 fusion.14
  282.3 2.4 fusion.30
  284.7 0.0 collective-permute-done.2
  284.7 0.0 copy-start.2
  284.7 2.9 copy-done.2
  287.6 1.4 copy.11
  289.0 0.0 collective-permute-done.3
  289.0 7.6 %copy.13 = f32[8,15,1,120,128]{4,1,3,0,2:T(8,128)} copy(f32[8,15,1,120,128]{4,3,2,1,0:T(8,128)} %collective-permute-done.3) | data formatting | bytes 14745600 | tf_op jit(solution)/shard_map/ppermute | solution.py:15
  296.7 30.1 %select_maximum_fusion = f32[8,15,3,122,130]{4,1,3,0,2:T(8,128)} fusion(f32[8,15,1,120,128]{4,1,3,0,2:T(8,128)} %copy.13, f32[8,15,1,120,128]{4,1,3,0,2:T(8,128)S(1)} %copy.11, f32[7,15,1,120,128]{4,1,3,0,2:T(8,128)S(1)} %fusion.18, f32[1,15,1,120,128]{4,1,3,0,2:T(8,128)S(1)} %bitcast.48), kind=kLoop, calls=%fused_computation.4 | loop fusion | flops 102772800 | bytes 44956800 | tf_op jit(solution)/shard_map/concatenate | solution.py:16
  326.7 0.0 copy-start.1
  326.8 25.5 %fusion.5 = f32[15,120,128]{2,0,1:T(8,128)S(1)} fusion(f32[8,15,3,122,130]{4,1,3,0,2:T(8,128)} %select_maximum_fusion, f32[8,120,128]{2,1,0:T(8,128)} %get-tuple-element.10, f32[8,120,128]{2,1,0:T(8,128)} %get-tuple-element.6, f32[8,120,128]{2,1,0:T(8,128)} %get-tuple-element.7, f32[8,120,128]{2,1,0:T(8,128)} %get-tuple-element.8, ...), kind=kLoop, calls=%fused_computation.13 | loop fusion | flops 34790400 | bytes 55480320 | tf_op jit(solution)/shard_map/reduce_sum | solution.py:61
  352.3 1.2 copy.16
  353.5 0.0 copy-done.1
  (1 shorter events, 0.0 us)
Async XLA Ops:
  6.5 164.0 %copy-start = (f32[7,120,120]{2,1,0:T(8,128)S(1)}, f32[7,120,120]{2,1,0:T(8,128)}, u32[]{:S(2)}) copy-start(f32[7,120,120]{2,1,0:T(8,128)} %param.7) | copy-start | bytes 1209604
  6.5 164.0 %all-gather.2.cloned.1.call-start = ((), (), s32[]{:S(2)}) async-start(), calls=%async_computation | async-start | bytes 8294400 | tf_op jit(solution)/shard_map/all_gather | solution.py:53
  182.0 11.2 %copy-start.3 = (f32[7,1,120,128]{3,2,1,0:T(8,128)S(1)}, f32[7,1,120,128]{3,2,1,0:T(8,128)}, u32[]{:S(2)}) copy-start(f32[7,1,120,128]{3,2,1,0:T(8,128)} %param.6) | copy-start | bytes 1290244
  182.0 11.2 %copy-start.4 = (f32[1,120,128]{2,1,0:T(8,128)S(1)}, f32[1,120,128]{2,1,0:T(8,128)}, u32[]{:S(2)}) copy-start(f32[1,120,128]{2,1,0:T(8,128)} %param.5) | copy-start | bytes 184324
  187.2 97.5 %collective-permute-start.2 = (f32[8,15,1,120,128]{4,3,2,1,0:T(8,128)}, f32[8,15,1,120,128]{4,3,2,1,0:T(8,128)S(1)}, u32[]{:S(2)}, u32[]{:S(2)}) collective-permute-start(f32[8,15,1,120,128]{4,3,2,1,0:T(8,128)} %copy.10), channel_id=1, source_target_pairs={{0,1},{1,2},{2,3},{3,4},{4,5},{5,6},{6,7},{7,8},{8,9},{9,10},{10,1... | collective-permute-start | bytes 22118408 | tf_op jit(solution)/shard_map/ppermute | solution.py:12
  191.3 97.8 %collective-permute-start.3 = (f32[8,15,1,120,128]{4,3,2,1,0:T(8,128)}, f32[8,15,1,120,128]{4,3,2,1,0:T(8,128)}, u32[]{:S(2)}, u32[]{:S(2)}) collective-permute-start(f32[8,15,1,120,128]{4,3,2,1,0:T(8,128)} %copy.10), channel_id=1, source_target_pairs={{1,0},{2,1},{3,2},{4,3},{5,4},{6,5},{7,6},{8,7},{9,8},{10,9},{11,1... | collective-permute-start | bytes 22118408 | tf_op jit(solution)/shard_map/ppermute | solution.py:15
  193.3 83.0 %collective-permute-start = (f32[8,1,120,128]{3,2,1,0:T(8,128)S(1)}, f32[8,1,120,128]{3,2,1,0:T(8,128)S(1)}, u32[]{:S(2)}, u32[]{:S(2)}) collective-permute-start(f32[8,1,120,128]{3,2,1,0:T(8,128)S(1)} %pad_maximum_fusion.1), channel_id=1, source_target_pairs={{0,1},{1,2},{2,3},{3,4},{4,5},{5,6},{6,7},{7,8},{8,9},{9,10},{10,1... | collective-permute-start | bytes 1474568 | tf_op jit(solution)/shard_map/ppermute | solution.py:12
  196.9 83.7 %collective-permute-start.1 = (f32[8,1,120,128]{3,2,1,0:T(8,128)S(1)}, f32[8,1,120,128]{3,2,1,0:T(8,128)S(1)}, u32[]{:S(2)}, u32[]{:S(2)}) collective-permute-start(f32[8,1,120,128]{3,2,1,0:T(8,128)S(1)} %pad_maximum_fusion.1), channel_id=1, source_target_pairs={{1,0},{2,1},{3,2},{4,3},{5,4},{6,5},{7,6},{8,7},{9,8},{10,9},{11,1... | collective-permute-start | bytes 1474568 | tf_op jit(solution)/shard_map/ppermute | solution.py:15
  284.7 2.9 copy-start.2
  326.7 26.7 %copy-start.1 = (f32[7,120,120]{2,1,0:T(8,128)S(1)}, f32[7,120,120]{2,1,0:T(8,128)}, u32[]{:S(2)}) copy-start(f32[7,120,120]{2,1,0:T(8,128)} %param.7) | copy-start | bytes 1209604
Sparse Core Ops, SparseCore 0:
  10.0 160.4 all-gather.1
where the time goes:
time: 361 us; the launch traced here: 360 us
  waiting for transfers between devices  244 us (68%)
  other arithmetic  60.3 us (17%)
  local copies, waits for them, and re-layouts  19.7 us (5%)
  between operations  13.5 us (4%)
  starting transfers between devices  11.7 us (3%)
  matrix products  10.9 us (3%)
    all_gather x1, waiting for transfers between devices, local(): block_piece = lax.all_gather(mode_coeffs, 'modes', axis=0, tiled=True)  162 us
    ppermute x2, waiting for transfers between devices, extended(): lax.ppermute(lax.slice_in_dim(block, block.shape[dim] - width, None, axis...  77.2 us
    concatenate x1, other arithmetic, extended(): block = jnp.concatenate([low, block, high], axis=dim)  30.1 us
    reduce_sum x1, other arithmetic, local(): return jnp.sum(operate(field_pad, perm_pad), axis=0)  25.5 us
    dot_general x1, matrix products, local(): jnp.einsum('kin,nc->kic', own_rows, flat_piece, precision=lax.Precision.H...  10.9 us
    ppermute x2, starting transfers between devices, extended(): lax.ppermute(lax.slice_in_dim(block, block.shape[dim] - width, None, axis...  7.72 us
    ppermute x1, local copies, waits for them, and re-layouts, extended(): lax.ppermute(lax.slice_in_dim(block, 0, width, axis=dim), axis, backward)  7.63 us
  transfers between devices with their start and end apart: 5, of which 3 were waited for; matrix products, arithmetic and copies ran while one was open for 2% of the time, Pallas kernels for 0%

commit v1 on v0

v1 whole, which is shorter than its diff:
```python
import functools

import jax
import jax.numpy as jnp
from jax import lax
from jax.experimental import pallas as pl
from jax.experimental.pallas import tpu as pltpu
from jax.sharding import PartitionSpec as P

MESH = pl.DeviceIdType.MESH
F32, BF16 = jnp.float32, jnp.bfloat16

MD = 15
MP = 16
NX = 4
NY, NZ = 120, 128
KT = 8
R = 8
NC = NY // R
AHEAD = 3
OUT2 = 2 * MP
PR = NY + 16
KD = 3 * NX * MP


def kernel(u, mean, kl, cpl, out, gath, fld, flo, fhi, cplv, cf, w, part, tlo, thi, hlo, hhi, zr,
           carry, sem_l, sx_s, sx_r, sf_s, sh_s, sh_r, sz_s, sz_r, ff_s, ff_r):
    m = lax.axis_index("modes")
    s = lax.axis_index("space")
    x = lax.rem(m, NX)
    zhi = m // NX
    first, last = s == 0, s == 31
    xr = zhi * NX + lax.rem(x + 1, NX)
    xl = zhi * NX + lax.rem(x + NX - 1, NX)
    zp = lax.rem(m + NX, 2 * NX)

    barrier = pltpu.get_barrier_semaphore()

    def greet(dev):
        pl.semaphore_signal(barrier, inc=1, device_id=dev, device_id_type=MESH)

    greet((xr, s))
    greet((xl, s))
    greet((zp, s))

    @pl.when(jnp.logical_not(first))
    def _():
        greet((m, s - 1))

    @pl.when(jnp.logical_not(last))
    def _():
        greet((m, s + 1))

    local = [
        pltpu.make_async_copy(u, gath.at[x, 0:MD], sem_l.at[0]),
        pltpu.make_async_copy(mean, fld.at[0], sem_l.at[1]),
        pltpu.make_async_copy(kl, fld.at[1:KT], sem_l.at[2]),
        pltpu.make_async_copy(cpl, cplv, sem_l.at[3]),
    ]
    for copy in local:
        copy.start()

    gath[:, MD] = jnp.zeros((NX, NY, NZ), F32)

    @pl.when(first)
    def _():
        flo[...] = jnp.zeros(flo.shape, F32)
        hlo[...] = jnp.zeros(hlo.shape, F32)

    @pl.when(last)
    def _():
        fhi[...] = jnp.zeros(fhi.shape, F32)
        hhi[...] = jnp.zeros(hhi.shape, F32)

    carry[...] = jnp.zeros(carry.shape, F32)

    pl.semaphore_wait(barrier, 5 - first.astype(jnp.int32) - last.astype(jnp.int32))

    def remote(src, dst, send, recv, dev):
        return pltpu.make_async_remote_copy(
            src_ref=src, dst_ref=dst, send_sem=send, recv_sem=recv, device_id=dev, device_id_type=MESH
        )

    def rows(c, base=0):
        return pl.ds(pl.multiple_of(base + c * R, R), R)

    def own_right(c):
        return remote(u.at[:, rows(c)], gath.at[x, 0:MD, rows(c)], sx_s.at[0, c], sx_r.at[0, c], (xr, s))

    def own_left(c):
        return remote(u.at[:, rows(c)], gath.at[x, 0:MD, rows(c)], sx_s.at[1, c], sx_r.at[1, c], (xl, s))

    x_l, x_r = lax.rem(x + NX - 1, NX), lax.rem(x + 1, NX)

    def got_left(c):
        return remote(u.at[:, rows(c)], gath.at[x_l, 0:MD, rows(c)], sx_s.at[0, c], sx_r.at[0, c], (xr, s))

    def got_right(c):
        return remote(u.at[:, rows(c)], gath.at[x_r, 0:MD, rows(c)], sx_s.at[1, c], sx_r.at[1, c], (xl, s))

    def on_right(c):
        ref = gath.at[x_l, 0:MD, rows(c)]
        return remote(ref, ref, sf_s.at[c], sx_r.at[2, c], (xr, s))

    def on_left(c):
        ref = gath.at[x_r, 0:MD, rows(c)]
        return remote(ref, ref, sf_s.at[c], sx_r.at[2, c], (xl, s))

    def got_far(c):
        ref = gath.at[lax.rem(x + 2, NX), 0:MD, rows(c)]
        return remote(ref, ref, sf_s.at[c], sx_r.at[2, c], (xr, s))

    def fields(i, dev, dst):
        return [
            remote(mean, dst.at[0], ff_s.at[i, 0], ff_r.at[i, 0], dev),
            remote(kl, dst.at[1:KT], ff_s.at[i, 1], ff_r.at[i, 1], dev),
        ]

    up_f = fields(0, (m, s + 1), flo)
    down_f = fields(1, (m, s - 1), fhi)

    def halo_up(c):
        return remote(thi.at[:, 0:MD, rows(c)], hlo.at[:, 0:MD, rows(c)], sh_s.at[0, c], sh_r.at[0, c], (m, s + 1))

    def halo_down(c):
        return remote(tlo.at[:, 0:MD, rows(c)], hhi.at[:, 0:MD, rows(c)], sh_s.at[1, c], sh_r.at[1, c], (m, s - 1))

    def across(c):
        return remote(part.at[1, 0:MD, rows(c, R)], zr.at[:, rows(c)], sz_s.at[c], sz_r.at[c], (zp, s))

    @pl.when(jnp.logical_not(last))
    def _():
        for copy in up_f:
            copy.start()

    @pl.when(jnp.logical_not(first))
    def _():
        for copy in down_f:
            copy.start()

    for c in range(AHEAD):
        own_right(c).start()
        own_left(c).start()

    local[3].wait()
    ri = lax.broadcasted_iota(jnp.int32, (OUT2, NY), 0)
    rc = lax.broadcasted_iota(jnp.int32, (OUT2, NY), 1)
    ro, rm = ri // MP, lax.rem(ri, MP)
    row_of = jnp.where(ro == 0, m, zp) * MD + rm
    pick = jnp.where((rc == row_of) & (rm < MD), 1.0, 0.0).astype(BF16)
    ci = lax.broadcasted_iota(jnp.int32, (NY, KD), 0)
    cj = lax.broadcasted_iota(jnp.int32, (NY, KD), 1)
    blk, cs = cj // (NX * MP), lax.rem(cj, NX * MP)
    cm = lax.rem(cs, MP)
    hit = (ci == zhi * (NX * MD) + (cs // MP) * MD + cm) & (cm < MD)
    put_hi = jnp.where(hit & (blk < 2), 1.0, 0.0).astype(BF16)
    put_lo = jnp.where(hit & (blk == 2), 1.0, 0.0).astype(BF16)
    di = lax.broadcasted_iota(jnp.int32, (OUT2, KD), 0)
    dj = lax.broadcasted_iota(jnp.int32, (OUT2, KD), 1)
    same = (di < MD) & (dj < 2 * NX * MP) & (lax.rem(dj, NX * MP) == x * MP + di)
    w[0:OUT2] = jnp.where(same, 1.0, 0.0).astype(BF16)

    def dot(a, b):
        return jnp.dot(a, b, preferred_element_type=F32)

    for k in range(1, KT):
        full = cplv[k - 1]
        hi = full.astype(BF16)
        lo = (full - hi.astype(F32)).astype(BF16)
        rows_hi = dot(pick, hi).astype(BF16)
        rows_lo = dot(pick, lo).astype(BF16)
        w[k * OUT2:(k + 1) * OUT2] = (dot(rows_hi, put_hi) + dot(rows_lo, put_lo)).astype(BF16)

    local[1].wait()
    local[2].wait()
    lane = lax.broadcasted_iota(jnp.int32, (NY, NZ), 1)
    none = jnp.zeros((1, NZ), F32)
    for k in range(KT):
        a = fld[k]
        cf[2, k, 0:NY + 1] = 0.5 * (jnp.concatenate([none, a], 0) + jnp.concatenate([a, none], 0))
        cf[3, k, 0:NY] = 0.5 * (a + jnp.where(lane == 0, 0.0, pltpu.roll(a, 1, 1)))
        cf[4, k, 0:NY] = 0.5 * (a + jnp.where(lane == NZ - 1, 0.0, pltpu.roll(a, NZ - 1, 1)))

    @pl.when(jnp.logical_not(first))
    def _():
        for copy in up_f:
            copy.wait_recv()

    @pl.when(jnp.logical_not(last))
    def _():
        for copy in down_f:
            copy.wait_recv()

    for k in range(KT):
        cf[0, k, 0:NY] = 0.5 * (fld[k] + flo[k])
        cf[1, k, 0:NY] = 0.5 * (fld[k] + fhi[k])

    local[0].wait()

    gflat = gath.reshape(NX * MP * NY, NZ)
    pflat = part.reshape(OUT2 * PR, NZ)
    tlo_flat = tlo.reshape(OUT2 * NY, NZ)
    thi_flat = thi.reshape(OUT2 * NY, NZ)
    lane2 = lax.broadcasted_iota(jnp.int32, (OUT2, NZ), 1)

    def compute(c):
        def pair(q, held):
            acc, above = held
            r0 = c * R + 2 * q
            cols = []
            for a in range(2):
                xf = gflat[pl.ds(r0 + a, NX * MP, stride=NY), :]
                hi = xf.astype(BF16)
                lo = (xf - hi.astype(F32)).astype(BF16)
                cols.append(jnp.concatenate([hi, lo, hi], 0))
            v = dot(w[...], jnp.concatenate(cols, 1))
            for a in range(2):
                r = r0 + a
                sums = [None] * 6
                for k in range(KT):
                    vk = v[k * OUT2:(k + 1) * OUT2, a * NZ:(a + 1) * NZ]
                    for d, (kind, at) in enumerate(((0, 0), (1, 0), (2, 0), (2, 1), (3, 0), (4, 0))):
                        term = cf[kind, k, pl.ds(r + at, 1), :] * vk
                        sums[d] = term if sums[d] is None else sums[d] + term
                xlo, xhi, ylo, yhi, zlo, zhi_ = sums
                tlo_flat[pl.ds(r, OUT2, stride=NY), :] = xlo
                thi_flat[pl.ds(r, OUT2, stride=NY), :] = xhi
                pflat[pl.ds(r + R - 1, OUT2, stride=PR), :] = acc - ylo
                acc = ((xlo + xhi) + (ylo + yhi)) + (zlo + zhi_) - above
                acc = acc - jnp.where(lane2 == 0, 0.0, pltpu.roll(zhi_, 1, 1))
                acc = acc - jnp.where(lane2 == NZ - 1, 0.0, pltpu.roll(zlo, NZ - 1, 1))
                above = yhi
            return acc, above

        acc, above = lax.fori_loop(0, R // 2, pair, (carry[0], carry[1]))
        carry[0] = acc
        carry[1] = above

    def step(t, _):
        @pl.when(t + AHEAD < NC)
        def _():
            own_right(t + AHEAD).start()
            own_left(t + AHEAD).start()

        @pl.when(t < NC)
        def _():
            got_left(t).wait_recv()
            got_right(t).wait_recv()

            @pl.when(lax.rem(t, 2) == 0)
            def _():
                on_right(t).start()

            @pl.when(lax.rem(t, 2) == 1)
            def _():
                on_left(t).start()

        @pl.when((t >= 1) & (t < NC + 1))
        def _():
            c = t - 1
            got_far(c).wait_recv()
            compute(c)

            @pl.when(jnp.logical_not(last))
            def _():
                halo_up(c).start()

            @pl.when(jnp.logical_not(first))
            def _():
                halo_down(c).start()

            @pl.when(c == NC - 1)
            def _():
                pflat[pl.ds(NY - 1 + R, OUT2, stride=PR), :] = carry[0]

        @pl.when(t >= 2)
        def _():
            c = t - 2

            @pl.when(jnp.logical_not(first))
            def _():
                halo_up(c).wait_recv()

            @pl.when(jnp.logical_not(last))
            def _():
                halo_down(c).wait_recv()

            part[:, 0:MD, rows(c, R)] = part[:, 0:MD, rows(c, R)] - (hlo[:, 0:MD, rows(c)] + hhi[:, 0:MD, rows(c)])
            across(c).start()

        return 0

    lax.fori_loop(0, NC + 2, step, 0)

    def finish(c, _):
        across(c).wait_recv()
        out[:, rows(c)] = part[0, 0:MD, rows(c, R)] + zr[:, rows(c)]
        return 0

    lax.fori_loop(0, NC, finish, 0)

    def drain(c, _):
        own_right(c).wait_send()
        own_left(c).wait_send()
        on_right(c).wait_send()
        across(c).wait_send()

        @pl.when(jnp.logical_not(last))
        def _():
            halo_up(c).wait_send()

        @pl.when(jnp.logical_not(first))
        def _():
            halo_down(c).wait_send()

        return 0

    lax.fori_loop(0, NC, drain, 0)

    @pl.when(jnp.logical_not(last))
    def _():
        for copy in up_f:
            copy.wait_send()

    @pl.when(jnp.logical_not(first))
    def _():
        for copy in down_f:
            copy.wait_send()


def local(mode_coeffs, mean_perm, kl_fields, couplings):
    dma = pltpu.SemaphoreType.DMA
    hbm = pl.BlockSpec(memory_space=pl.ANY)
    vmem = pltpu.VMEM
    res = pl.pallas_call(
        kernel,
        out_shape=jax.ShapeDtypeStruct((MD, NY, NZ), F32),
        in_specs=[hbm] * 4,
        out_specs=pl.BlockSpec(memory_space=pltpu.VMEM),
        scratch_shapes=[
            vmem((NX, MP, NY, NZ), F32),
            vmem((KT, NY, NZ), F32),
            vmem((KT, NY, NZ), F32),
            vmem((KT, NY, NZ), F32),
            vmem((KT - 1, NY, NY), F32),
            vmem((5, KT, 128, NZ), F32),
            vmem((KT * OUT2, KD), BF16),
            vmem((2, MP, PR, NZ), F32),
            vmem((2, MP, NY, NZ), F32),
            vmem((2, MP, NY, NZ), F32),
            vmem((2, MP, NY, NZ), F32),
            vmem((2, MP, NY, NZ), F32),
            vmem((MD, NY, NZ), F32),
            vmem((2, OUT2, NZ), F32),
            dma((4,)),
            dma((2, NC)), dma((3, NC)), dma((NC,)),
            dma((2, NC)), dma((2, NC)),
            dma((NC,)), dma((NC,)),
            dma((2, 2)), dma((2, 2)),
        ],
        compiler_params=pltpu.CompilerParams(
            collective_id=0, has_side_effects=True, vmem_limit_bytes=56 * 1024 * 1024
        ),
    )(mode_coeffs.reshape(MD, NY, NZ), mean_perm.reshape(NY, NZ), kl_fields.reshape(KT - 1, NY, NZ), couplings)
    return res.reshape(MD, 1, NY, NZ)


def solution(mesh):
    in_specs = (
        P("modes", "space", None, None),
        P("space", None, None),
        P(None, "space", None, None),
        P(),
    )
    out_specs = P("modes", "space", None, None)
    return jax.shard_map(local, mesh=mesh, in_specs=in_specs, out_specs=out_specs, check_vma=False)
```

time: 361 us -> 96.3 us (0.27)
  the two profiles are of different devices: /device:TPU:1 before, /device:TPU:192 now
where the time goes in v1:
time: 96.3 us; the launch traced here: 96.2 us
  Pallas kernels  94 us (98%)
  local copies, waits for them, and re-layouts  2.16 us (2%)
    pallas_call x1, Pallas kernels, local(): pl.pallas_call(kernel, out_shape=jax.ShapeDtypeStruct((MD, NY, NZ), F32),...  94 us
    unnamed x1, local copies, waits for them, and re-layouts  2.16 us

profile of v1, /device:TPU:192, one launch (start us, length us, event | category | flops | bytes accessed | tf_op | source)
XLA Modules:
  0.0 96.2 jit_solution(9106550899899857212)
XLA Ops:
  0.0 94.0 %shard_map.46 = f32[15,120,128]{2,1,0:T(8,128)} custom-call(f32[15,120,128]{2,1,0:T(8,128)} %bitcast.7, f32[120,128]{1,0:T(8,128)} %bitcast.9, f32[7,120,128]{2,1,0:T(8,128)} %bitcast.8, f32[7,120,120]{2,1,0:T(8,128)} %cpl.1), custom_call_target="tpu_custom_call" | custom-call | tf_op jit(solution)/shard_map/pallas_call | solution.py:335
  94.0 2.2 %copy.7 = f32[15,1,120,128]{3,2,1,0:T(8,128)} copy(f32[15,1,120,128]{3,2,1,0:T(8,128)} %bitcast.6) | data formatting | bytes 1843200

commit v2 on v1

--- a/solution.py
+++ b/solution.py
@@ -17,14 +17,15 @@
 KT = 8
 R = 8
 NC = NY // R
-AHEAD = 3
+LINE = 8
 OUT2 = 2 * MP
 PR = NY + 16
 KD = 3 * NX * MP
-
-
-def kernel(u, mean, kl, cpl, out, gath, fld, flo, fhi, cplv, cf, w, part, tlo, thi, hlo, hhi, zr,
-           carry, sem_l, sx_s, sx_r, sf_s, sh_s, sh_r, sz_s, sz_r, ff_s, ff_r):
+LAG = 4
+
+
+def kernel(u, mean, kl, cpl, out, zr, gath, fld, flo, fhi, rfl, cplv, cf, w, part, tlo, thi, hlo, hhi, rel,
+           carry, sem_l, sem_o, sx_s, sx_r, sh_s, sh_r, sr_s, sr_r, sz_s, sz_r, ff_s, ff_r, fr_s, fr_r):
     m = lax.axis_index("modes")
     s = lax.axis_index("space")
     x = lax.rem(m, NX)
@@ -34,6 +35,20 @@
     xl = zhi * NX + lax.rem(x + NX - 1, NX)
     zp = lax.rem(m + NX, 2 * NX)
 
+    xf = zhi * NX + lax.rem(x + 2, NX)
+
+    y, core, zlo = lax.rem(s, LINE) // 2, lax.rem(s, 2), s // LINE
+    line = zlo * LINE
+    up, down = jnp.logical_not(last), jnp.logical_not(first)
+    seam_up = (core == 1) & (y == 3) & (zlo < 3)
+    seam_down = (core == 0) & (y == 0) & (zlo > 0)
+    relay_up = (core == 1) & (y == 0) & (zlo < 3)
+    relay_down = (core == 0) & (y == 3) & (zlo > 0)
+    seam, relay = seam_up | seam_down, relay_up | relay_down
+    goal = jnp.where(core == 1, line + LINE, line - 1)
+    origin = jnp.where(core == 1, line + LINE - 1, line)
+    aside = jnp.where(core == 1, line + 1, line + LINE - 2)
+
     barrier = pltpu.get_barrier_semaphore()
 
     def greet(dev):
@@ -41,15 +56,30 @@
 
     greet((xr, s))
     greet((xl, s))
+    greet((xf, s))
     greet((zp, s))
 
-    @pl.when(jnp.logical_not(first))
+    @pl.when(down)
     def _():
         greet((m, s - 1))
 
-    @pl.when(jnp.logical_not(last))
+    @pl.when(up)
     def _():
         greet((m, s + 1))
+
+    @pl.when(relay)
+    def _():
+        greet((m, origin))
+
+    @pl.when(seam_down)
+    def _():
+        greet((m, line - LINE + 1))
+        greet((m, aside))
+
+    @pl.when(seam_up)
+    def _():
+        greet((m, line + LINE + LINE - 2))
+        greet((m, aside))
 
     local = [
         pltpu.make_async_copy(u, gath.at[x, 0:MD], sem_l.at[0]),
@@ -74,7 +104,8 @@
 
     carry[...] = jnp.zeros(carry.shape, F32)
 
-    pl.semaphore_wait(barrier, 5 - first.astype(jnp.int32) - last.astype(jnp.int32))
+    one = jnp.int32
+    pl.semaphore_wait(barrier, 4 + up.astype(one) + down.astype(one) + 2 * relay.astype(one) + seam.astype(one))
 
     def remote(src, dst, send, recv, dev):
         return pltpu.make_async_remote_copy(
@@ -84,40 +115,33 @@
     def rows(c, base=0):
         return pl.ds(pl.multiple_of(base + c * R, R), R)
 
-    def own_right(c):
-        return remote(u.at[:, rows(c)], gath.at[x, 0:MD, rows(c)], sx_s.at[0, c], sx_r.at[0, c], (xr, s))
-
-    def own_left(c):
-        return remote(u.at[:, rows(c)], gath.at[x, 0:MD, rows(c)], sx_s.at[1, c], sx_r.at[1, c], (xl, s))
-
-    x_l, x_r = lax.rem(x + NX - 1, NX), lax.rem(x + 1, NX)
-
-    def got_left(c):
-        return remote(u.at[:, rows(c)], gath.at[x_l, 0:MD, rows(c)], sx_s.at[0, c], sx_r.at[0, c], (xr, s))
-
-    def got_right(c):
-        return remote(u.at[:, rows(c)], gath.at[x_r, 0:MD, rows(c)], sx_s.at[1, c], sx_r.at[1, c], (xl, s))
-
-    def on_right(c):
-        ref = gath.at[x_l, 0:MD, rows(c)]
-        return remote(ref, ref, sf_s.at[c], sx_r.at[2, c], (xr, s))
-
-    def on_left(c):
-        ref = gath.at[x_r, 0:MD, rows(c)]
-        return remote(ref, ref, sf_s.at[c], sx_r.at[2, c], (xl, s))
-
-    def got_far(c):
-        ref = gath.at[lax.rem(x + 2, NX), 0:MD, rows(c)]
-        return remote(ref, ref, sf_s.at[c], sx_r.at[2, c], (xr, s))
-
-    def fields(i, dev, dst):
-        return [
-            remote(mean, dst.at[0], ff_s.at[i, 0], ff_r.at[i, 0], dev),
-            remote(kl, dst.at[1:KT], ff_s.at[i, 1], ff_r.at[i, 1], dev),
-        ]
-
-    up_f = fields(0, (m, s + 1), flo)
-    down_f = fields(1, (m, s - 1), fhi)
+    x_from = [lax.rem(x + NX - 1, NX), lax.rem(x + 1, NX), lax.rem(x + 2, NX)]
+    x_to = [xr, xl, xf]
+
+    def own(i, c):
+        return remote(u.at[:, rows(c)], gath.at[x, 0:MD, rows(c)], sx_s.at[i, c], sx_r.at[i, c], (x_to[i], s))
+
+    def got(i, c):
+        ref = gath.at[x_from[i], 0:MD, rows(c)]
+        return remote(ref, ref, sx_s.at[i, c], sx_r.at[i, c], (x_to[i], s))
+
+    def field(k):
+        return mean if k == 0 else kl.at[k - 1]
+
+    def field_up(k):
+        return remote(field(k), flo.at[k], ff_s.at[0, k], ff_r.at[0, k], (m, s + 1))
+
+    def field_down(k):
+        return remote(field(k), fhi.at[k], ff_s.at[1, k], ff_r.at[1, k], (m, s - 1))
+
+    def field_aside(k):
+        return remote(field(k), rfl.at[k], ff_s.at[core ^ 1, k], fr_r.at[k], (m, aside))
+
+    def field_relay_up(k):
+        return remote(rfl.at[k], flo.at[k], fr_s.at[k], ff_r.at[0, k], (m, goal))
+
+    def field_relay_down(k):
+        return remote(rfl.at[k], fhi.at[k], fr_s.at[k], ff_r.at[1, k], (m, goal))
 
     def halo_up(c):
         return remote(thi.at[:, 0:MD, rows(c)], hlo.at[:, 0:MD, rows(c)], sh_s.at[0, c], sh_r.at[0, c], (m, s + 1))
@@ -125,22 +149,43 @@
     def halo_down(c):
         return remote(tlo.at[:, 0:MD, rows(c)], hhi.at[:, 0:MD, rows(c)], sh_s.at[1, c], sh_r.at[1, c], (m, s - 1))
 
+    def aside_up(c):
+        return remote(thi.at[:, 0:MD, rows(c)], rel.at[:, 0:MD, rows(c)], sh_s.at[0, c], sr_r.at[c],
+                      (m, aside))
+
+    def aside_down(c):
+        return remote(tlo.at[:, 0:MD, rows(c)], rel.at[:, 0:MD, rows(c)], sh_s.at[1, c], sr_r.at[c],
+                      (m, aside))
+
+    def relay_on_up(c):
+        return remote(rel.at[:, 0:MD, rows(c)], hlo.at[:, 0:MD, rows(c)], sr_s.at[c], sh_r.at[0, c], (m, goal))
+
+    def relay_on_down(c):
+        return remote(rel.at[:, 0:MD, rows(c)], hhi.at[:, 0:MD, rows(c)], sr_s.at[c], sh_r.at[1, c], (m, goal))
+
     def across(c):
         return remote(part.at[1, 0:MD, rows(c, R)], zr.at[:, rows(c)], sz_s.at[c], sz_r.at[c], (zp, s))
 
-    @pl.when(jnp.logical_not(last))
-    def _():
-        for copy in up_f:
-            copy.start()
-
-    @pl.when(jnp.logical_not(first))
-    def _():
-        for copy in down_f:
-            copy.start()
-
-    for c in range(AHEAD):
-        own_right(c).start()
-        own_left(c).start()
+    def keep(c):
+        return pltpu.make_async_copy(part.at[0, 0:MD, rows(c, R)], out.at[:, rows(c)], sem_o.at[c])
+
+    def when(cond, fn):
+        pl.when(cond)(fn)
+
+    for k in range(KT):
+        direct_up, direct_down = up, down
+        if k % 2 == 0:
+            direct_up, direct_down = up & jnp.logical_not(seam_up), down & jnp.logical_not(seam_down)
+            when(seam, lambda: field_aside(k).start())
+        when(direct_up, lambda: field_up(k).start())
+        when(direct_down, lambda: field_down(k).start())
+
+    def gather(c, _):
+        for i in range(3):
+            own(i, c).start()
+        return 0
+
+    lax.fori_loop(0, NC, gather, 0)
 
     local[3].wait()
     ri = lax.broadcasted_iota(jnp.int32, (OUT2, NY), 0)
@@ -181,15 +226,16 @@
         cf[3, k, 0:NY] = 0.5 * (a + jnp.where(lane == 0, 0.0, pltpu.roll(a, 1, 1)))
         cf[4, k, 0:NY] = 0.5 * (a + jnp.where(lane == NZ - 1, 0.0, pltpu.roll(a, NZ - 1, 1)))
 
-    @pl.when(jnp.logical_not(first))
-    def _():
-        for copy in up_f:
-            copy.wait_recv()
-
-    @pl.when(jnp.logical_not(last))
-    def _():
-        for copy in down_f:
-            copy.wait_recv()
+    for k in range(0, KT, 2):
+        @pl.when(relay)
+        def _():
+            field_aside(k).wait_recv()
+            when(core == 1, lambda: field_relay_up(k).start())
+            when(core == 0, lambda: field_relay_down(k).start())
+
+    for k in range(KT):
+        when(down, lambda: field_up(k).wait_recv())
+        when(up, lambda: field_down(k).wait_recv())
 
     for k in range(KT):
         cf[0, k, 0:NY] = 0.5 * (fld[k] + flo[k])
@@ -236,109 +282,85 @@
         carry[0] = acc
         carry[1] = above
 
+    def send_halos(c):
+        even = lax.rem(c, 2) == 0
+        off_up, off_down = seam_up & even, seam_down & even
+        when(up & jnp.logical_not(off_up), lambda: halo_up(c).start())
+        when(down & jnp.logical_not(off_down), lambda: halo_down(c).start())
+        when(off_up, lambda: aside_up(c).start())
+        when(off_down, lambda: aside_down(c).start())
+
+    def relays(c):
+        return relay & (lax.rem(c, 2) == 0)
+
     def step(t, _):
-        @pl.when(t + AHEAD < NC)
-        def _():
-            own_right(t + AHEAD).start()
-            own_left(t + AHEAD).start()
-
         @pl.when(t < NC)
         def _():
-            got_left(t).wait_recv()
-            got_right(t).wait_recv()
-
-            @pl.when(lax.rem(t, 2) == 0)
-            def _():
-                on_right(t).start()
-
-            @pl.when(lax.rem(t, 2) == 1)
-            def _():
-                on_left(t).start()
-
-        @pl.when((t >= 1) & (t < NC + 1))
+            for i in range(3):
+                got(i, t).wait_recv()
+
+        @pl.when((t >= 1) & (t <= NC) & relays(t + 1))
         def _():
             c = t - 1
-            got_far(c).wait_recv()
-            compute(c)
-
-            @pl.when(jnp.logical_not(last))
-            def _():
-                halo_up(c).start()
-
-            @pl.when(jnp.logical_not(first))
-            def _():
-                halo_down(c).start()
-
-            @pl.when(c == NC - 1)
+            aside_up(c).wait_recv()
+            when(core == 1, lambda: relay_on_up(c).start())
+            when(core == 0, lambda: relay_on_down(c).start())
+
+        @pl.when(t < NC)
+        def _():
+            compute(t)
+            send_halos(t)
+
+            @pl.when(t == NC - 1)
             def _():
                 pflat[pl.ds(NY - 1 + R, OUT2, stride=PR), :] = carry[0]
 
-        @pl.when(t >= 2)
+        @pl.when(t >= LAG)
         def _():
-            c = t - 2
-
-            @pl.when(jnp.logical_not(first))
-            def _():
-                halo_up(c).wait_recv()
-
-            @pl.when(jnp.logical_not(last))
-            def _():
-                halo_down(c).wait_recv()
-
+            c = t - LAG
+            when(down, lambda: halo_up(c).wait_recv())
+            when(up, lambda: halo_down(c).wait_recv())
             part[:, 0:MD, rows(c, R)] = part[:, 0:MD, rows(c, R)] - (hlo[:, 0:MD, rows(c)] + hhi[:, 0:MD, rows(c)])
             across(c).start()
+            keep(c).start()
 
         return 0
 
-    lax.fori_loop(0, NC + 2, step, 0)
-
-    def finish(c, _):
+    lax.fori_loop(0, NC + LAG, step, 0)
+
+    def drain(c, _):
+        for i in range(3):
+            own(i, c).wait_send()
+        when(up, lambda: halo_up(c).wait_send())
+        when(down, lambda: halo_down(c).wait_send())
+        when(relays(c), lambda: relay_on_up(c).wait_send())
+        keep(c).wait()
+        across(c).wait_send()
         across(c).wait_recv()
-        out[:, rows(c)] = part[0, 0:MD, rows(c, R)] + zr[:, rows(c)]
         return 0
 
-    lax.fori_loop(0, NC, finish, 0)
-
-    def drain(c, _):
-        own_right(c).wait_send()
-        own_left(c).wait_send()
-        on_right(c).wait_send()
-        across(c).wait_send()
-
-        @pl.when(jnp.logical_not(last))
-        def _():
-            halo_up(c).wait_send()
-
-        @pl.when(jnp.logical_not(first))
-        def _():
-            halo_down(c).wait_send()
-
-        return 0
+    for k in range(KT):
+        when(up, lambda: field_up(k).wait_send())
+        when(down, lambda: field_down(k).wait_send())
+        if k % 2 == 0:
+            when(relay, lambda: field_relay_up(k).wait_send())
 
     lax.fori_loop(0, NC, drain, 0)
-
-    @pl.when(jnp.logical_not(last))
-    def _():
-        for copy in up_f:
-            copy.wait_send()
-
-    @pl.when(jnp.logical_not(first))
-    def _():
-        for copy in down_f:
-            copy.wait_send()
 
 
 def local(mode_coeffs, mean_perm, kl_fields, couplings):
     dma = pltpu.SemaphoreType.DMA
     hbm = pl.BlockSpec(memory_space=pl.ANY)
     vmem = pltpu.VMEM
-    res = pl.pallas_call(
+    plane = jax.ShapeDtypeStruct((MD, NY, NZ), F32)
+    own, other = pl.pallas_call(
         kernel,
-        out_shape=jax.ShapeDtypeStruct((MD, NY, NZ), F32),
+        out_shape=(plane, plane),
         in_specs=[hbm] * 4,
-        out_specs=pl.BlockSpec(memory_space=pltpu.VMEM),
+        out_specs=(hbm, hbm),
         scratch_shapes=[
             vmem((NX, MP, NY, NZ), F32),
+            vmem((KT, NY, NZ), F32),
             vmem((KT, NY, NZ), F32),
             vmem((KT, NY, NZ), F32),
             vmem((KT, NY, NZ), F32),
@@ -350,19 +372,21 @@
             vmem((2, MP, NY, NZ), F32),
             vmem((2, MP, NY, NZ), F32),
             vmem((2, MP, NY, NZ), F32),
-            vmem((MD, NY, NZ), F32),
+            vmem((2, MP, NY, NZ), F32),
             vmem((2, OUT2, NZ), F32),
-            dma((4,)),
-            dma((2, NC)), dma((3, NC)), dma((NC,)),
+            dma((4,)), dma((NC,)),
+            dma((3, NC)), dma((3, NC)),
             dma((2, NC)), dma((2, NC)),
             dma((NC,)), dma((NC,)),
-            dma((2, 2)), dma((2, 2)),
+            dma((NC,)), dma((NC,)),
+            dma((2, KT)), dma((2, KT)),
+            dma((KT,)), dma((KT,)),
         ],
         compiler_params=pltpu.CompilerParams(
             collective_id=0, has_side_effects=True, vmem_limit_bytes=56 * 1024 * 1024
         ),
     )(mode_coeffs.reshape(MD, NY, NZ), mean_perm.reshape(NY, NZ), kl_fields.reshape(KT - 1, NY, NZ), couplings)
-    return res.reshape(MD, 1, NY, NZ)
+    return (own + other).reshape(MD, 1, NY, NZ)
 
 
 def solution(mesh):

time: 96.3 us -> 84.5 us (0.88)
  the two profiles are of different devices: /device:TPU:192 before, /device:TPU:1 now
where the time goes in v2:
time: 84.5 us; the launch traced here: 83.9 us
  Pallas kernels  81.5 us (96%)
  other arithmetic  2.47 us (3%)
    pallas_call x1, Pallas kernels, local(): pl.pallas_call(kernel, out_shape=(plane, plane), in_specs=[hbm] * 4, out_...  81.5 us
    reshape x1, other arithmetic, local(): return (own + other).reshape(MD, 1, NY, NZ)  2.47 us

profile of v2, /device:TPU:1, one launch (start us, length us, event | category | flops | bytes accessed | tf_op | source)
XLA Modules:
  0.0 83.9 jit_solution(16206326123101334395)
XLA Ops:
  0.0 81.5 %shard_map.46 = (f32[15,120,128]{2,1,0:T(8,128)}, f32[15,120,128]{2,1,0:T(8,128)}) custom-call(f32[15,120,128]{2,1,0:T(8,128)} %bitcast.7, f32[120,128]{1,0:T(8,128)} %bitcast.9, f32[7,120,128]{2,1,0:T(8,128)} %bitcast.8, f32[7,120,120]{2,1,0:T(8,128)} %cpl.1), custom_call_target="tpu_custom_call" | custom-call | tf_op jit(solution)/shard_map/pallas_call | solution.py:356
  81.5 2.5 %add_bitcast_fusion = f32[15,1,120,128]{3,2,1,0:T(8,128)} fusion(f32[15,120,128]{2,1,0:T(8,128)} %get-tuple-element.7, f32[15,120,128]{2,1,0:T(8,128)} %get-tuple-element.8), kind=kLoop, calls=%fused_computation | loop fusion | flops 230400 | bytes 2764800 | tf_op jit(solution)/shard_map/reshape | solution.py:389

commit v3 on v2

--- a/solution.py
+++ b/solution.py
@@ -21,7 +21,11 @@
 OUT2 = 2 * MP
 PR = NY + 16
 KD = 3 * NX * MP
-LAG = 4
+BACK = 2
+LATE = 4
+SEAM = 0
+AHEAD = 3
+LAG = 2
 
 
 def kernel(u, mean, kl, cpl, out, zr, gath, fld, flo, fhi, rfl, cplv, cf, w, part, tlo, thi, hlo, hhi, rel,
@@ -105,6 +109,7 @@
     carry[...] = jnp.zeros(carry.shape, F32)
 
     one = jnp.int32
+    lag = LAG + SEAM * seam.astype(one)
     pl.semaphore_wait(barrier, 4 + up.astype(one) + down.astype(one) + 2 * relay.astype(one) + seam.astype(one))
 
     def remote(src, dst, send, recv, dev):
@@ -143,25 +148,23 @@
     def field_relay_down(k):
         return remote(rfl.at[k], fhi.at[k], fr_s.at[k], ff_r.at[1, k], (m, goal))
 
-    def halo_up(c):
-        return remote(thi.at[:, 0:MD, rows(c)], hlo.at[:, 0:MD, rows(c)], sh_s.at[0, c], sh_r.at[0, c], (m, s + 1))
-
-    def halo_down(c):
-        return remote(tlo.at[:, 0:MD, rows(c)], hhi.at[:, 0:MD, rows(c)], sh_s.at[1, c], sh_r.at[1, c], (m, s - 1))
-
-    def aside_up(c):
-        return remote(thi.at[:, 0:MD, rows(c)], rel.at[:, 0:MD, rows(c)], sh_s.at[0, c], sr_r.at[c],
-                      (m, aside))
-
-    def aside_down(c):
-        return remote(tlo.at[:, 0:MD, rows(c)], rel.at[:, 0:MD, rows(c)], sh_s.at[1, c], sr_r.at[c],
-                      (m, aside))
-
-    def relay_on_up(c):
-        return remote(rel.at[:, 0:MD, rows(c)], hlo.at[:, 0:MD, rows(c)], sr_s.at[c], sh_r.at[0, c], (m, goal))
-
-    def relay_on_down(c):
-        return remote(rel.at[:, 0:MD, rows(c)], hhi.at[:, 0:MD, rows(c)], sr_s.at[c], sh_r.at[1, c], (m, goal))
+    def halo_up(o, c):
+        return remote(thi.at[o, 0:MD, rows(c)], hlo.at[o, 0:MD, rows(c)], sh_s.at[o, c], sh_r.at[o, c], (m, s + 1))
+
+    def halo_down(o, c):
+        return remote(tlo.at[o, 0:MD, rows(c)], hhi.at[o, 0:MD, rows(c)], sh_s.at[2 + o, c], sh_r.at[2 + o, c], (m, s - 1))
+
+    def aside_up(o, c):
+        return remote(thi.at[o, 0:MD, rows(c)], rel.at[o, 0:MD, rows(c)], sh_s.at[o, c], sr_r.at[o, c], (m, aside))
+
+    def aside_down(o, c):
+        return remote(tlo.at[o, 0:MD, rows(c)], rel.at[o, 0:MD, rows(c)], sh_s.at[2 + o, c], sr_r.at[o, c], (m, aside))
+
+    def relay_on_up(o, c):
+        return remote(rel.at[o, 0:MD, rows(c)], hlo.at[o, 0:MD, rows(c)], sr_s.at[o, c], sh_r.at[o, c], (m, goal))
+
+    def relay_on_down(o, c):
+        return remote(rel.at[o, 0:MD, rows(c)], hhi.at[o, 0:MD, rows(c)], sr_s.at[o, c], sh_r.at[2 + o, c], (m, goal))
 
     def across(c):
         return remote(part.at[1, 0:MD, rows(c, R)], zr.at[:, rows(c)], sz_s.at[c], sz_r.at[c], (zp, s))
@@ -185,7 +188,7 @@
             own(i, c).start()
         return 0
 
-    lax.fori_loop(0, NC, gather, 0)
+    lax.fori_loop(0, AHEAD, gather, 0)
 
     local[3].wait()
     ri = lax.broadcasted_iota(jnp.int32, (OUT2, NY), 0)
@@ -283,28 +286,35 @@
         carry[1] = above
 
     def send_halos(c):
-        even = lax.rem(c, 2) == 0
-        off_up, off_down = seam_up & even, seam_down & even
-        when(up & jnp.logical_not(off_up), lambda: halo_up(c).start())
-        when(down & jnp.logical_not(off_down), lambda: halo_down(c).start())
-        when(off_up, lambda: aside_up(c).start())
-        when(off_down, lambda: aside_down(c).start())
-
-    def relays(c):
-        return relay & (lax.rem(c, 2) == 0)
+        when(up, lambda: halo_up(1, c).start())
+        when(down, lambda: halo_down(1, c).start())
+        when(up & jnp.logical_not(seam_up), lambda: halo_up(0, c).start())
+        when(down & jnp.logical_not(seam_down), lambda: halo_down(0, c).start())
+        when(seam_up, lambda: aside_up(0, c).start())
+        when(seam_down, lambda: aside_down(0, c).start())
+
+    def join(o, c):
+        when(down, lambda: halo_up(o, c).wait_recv())
+        when(up, lambda: halo_down(o, c).wait_recv())
+        here = part[o, 0:MD, rows(c, R)]
+        part[o, 0:MD, rows(c, R)] = here - (hlo[o, 0:MD, rows(c)] + hhi[o, 0:MD, rows(c)])
 
     def step(t, _):
+        @pl.when(t + AHEAD < NC)
+        def _():
+            gather(t + AHEAD, 0)
+
         @pl.when(t < NC)
         def _():
             for i in range(3):
                 got(i, t).wait_recv()
 
-        @pl.when((t >= 1) & (t <= NC) & relays(t + 1))
-        def _():
-            c = t - 1
-            aside_up(c).wait_recv()
-            when(core == 1, lambda: relay_on_up(c).start())
-            when(core == 0, lambda: relay_on_down(c).start())
+        @pl.when((t >= BACK) & (t < NC + BACK) & relay)
+        def _():
+            c = t - BACK
+            aside_up(0, c).wait_recv()
+            when(core == 1, lambda: relay_on_up(0, c).start())
+            when(core == 0, lambda: relay_on_down(0, c).start())
 
         @pl.when(t < NC)
         def _():
@@ -315,26 +325,30 @@
             def _():
                 pflat[pl.ds(NY - 1 + R, OUT2, stride=PR), :] = carry[0]
 
-        @pl.when(t >= LAG)
-        def _():
-            c = t - LAG
-            when(down, lambda: halo_up(c).wait_recv())
-            when(up, lambda: halo_down(c).wait_recv())
-            part[:, 0:MD, rows(c, R)] = part[:, 0:MD, rows(c, R)] - (hlo[:, 0:MD, rows(c)] + hhi[:, 0:MD, rows(c)])
+        @pl.when((t >= lag) & (t < NC + lag))
+        def _():
+            c = t - lag
+            join(1, c)
             across(c).start()
+
+        @pl.when((t >= lag + LATE) & (t < NC + lag + LATE))
+        def _():
+            c = t - lag - LATE
+            join(0, c)
             keep(c).start()
 
         return 0
 
-    lax.fori_loop(0, NC + LAG, step, 0)
+    lax.fori_loop(0, NC + LAG + SEAM + LATE, step, 0)
 
     def drain(c, _):
         for i in range(3):
             own(i, c).wait_send()
-        when(up, lambda: halo_up(c).wait_send())
-        when(down, lambda: halo_down(c).wait_send())
-        when(relays(c), lambda: relay_on_up(c).wait_send())
+        for o in range(2):
+            when(up, lambda: halo_up(o, c).wait_send())
+            when(down, lambda: halo_down(o, c).wait_send())
         keep(c).wait()
+        when(relay, lambda: relay_on_up(0, c).wait_send())
         across(c).wait_send()
         across(c).wait_recv()
         return 0
@@ -376,8 +390,8 @@
             vmem((2, OUT2, NZ), F32),
             dma((4,)), dma((NC,)),
             dma((3, NC)), dma((3, NC)),
+            dma((4, NC)), dma((4, NC)),
             dma((2, NC)), dma((2, NC)),
-            dma((NC,)), dma((NC,)),
             dma((NC,)), dma((NC,)),
             dma((2, KT)), dma((2, KT)),
             dma((KT,)), dma((KT,)),

time: 84.5 us -> 82.1 us (0.972)
  Pallas kernels: 81.5 us -> 79.5 us
    pallas_call x1, Pallas kernels: 81.5 us -> 79.5 us  [local(): pl.pallas_call(kernel, out_shape=(plane, plane), in_specs=[hbm] * 4, out_...]
where the time goes in v3:
time: 82.1 us; the launch traced here: 82 us
  Pallas kernels  79.5 us (97%)
  other arithmetic  2.47 us (3%)
    pallas_call x1, Pallas kernels, local(): pl.pallas_call(kernel, out_shape=(plane, plane), in_specs=[hbm] * 4, out_...  79.5 us
    reshape x1, other arithmetic, local(): return (own + other).reshape(MD, 1, NY, NZ)  2.47 us

profile of v3, /device:TPU:1, one launch (start us, length us, event | category | flops | bytes accessed | tf_op | source)
XLA Modules:
  0.0 82.0 jit_solution(15858804609859149351)
XLA Ops:
  0.0 79.5 %shard_map.46 = (f32[15,120,128]{2,1,0:T(8,128)}, f32[15,120,128]{2,1,0:T(8,128)}) custom-call(f32[15,120,128]{2,1,0:T(8,128)} %bitcast.7, f32[120,128]{1,0:T(8,128)} %bitcast.9, f32[7,120,128]{2,1,0:T(8,128)} %bitcast.8, f32[7,120,120]{2,1,0:T(8,128)} %cpl.1), custom_call_target="tpu_custom_call" | custom-call | tf_op jit(solution)/shard_map/pallas_call | solution.py:370
  79.5 2.5 %add_bitcast_fusion = f32[15,1,120,128]{3,2,1,0:T(8,128)} fusion(f32[15,120,128]{2,1,0:T(8,128)} %get-tuple-element.7, f32[15,120,128]{2,1,0:T(8,128)} %get-tuple-element.8), kind=kLoop, calls=%fused_computation | loop fusion | flops 230400 | bytes 2764800 | tf_op jit(solution)/shard_map/reshape | solution.py:403

commit v4 on v3

--- a/solution.py
+++ b/solution.py
@@ -21,8 +21,8 @@
 OUT2 = 2 * MP
 PR = NY + 16
 KD = 3 * NX * MP
-BACK = 2
-LATE = 4
+BACK = 3
+LATE = 6
 SEAM = 0
 AHEAD = 3
 LAG = 2

time: 82.1 us -> 79.8 us (0.972)
  Pallas kernels: 79.5 us -> 76.5 us
    pallas_call x1, Pallas kernels: 79.5 us -> 76.5 us  [local(): pl.pallas_call(kernel, out_shape=(plane, plane), in_specs=[hbm] * 4, out_...]
where the time goes in v4:
time: 79.8 us; the launch traced here: 79 us
  Pallas kernels  76.5 us (96%)
  other arithmetic  2.47 us (3%)
    pallas_call x1, Pallas kernels, local(): pl.pallas_call(kernel, out_shape=(plane, plane), in_specs=[hbm] * 4, out_...  76.5 us
    reshape x1, other arithmetic, local(): return (own + other).reshape(MD, 1, NY, NZ)  2.47 us

profile of v4, /device:TPU:1, one launch (start us, length us, event | category | flops | bytes accessed | tf_op | source)
XLA Modules:
  0.0 79.0 jit_solution(17885877632145850811)
XLA Ops:
  0.0 76.5 %shard_map.46 = (f32[15,120,128]{2,1,0:T(8,128)}, f32[15,120,128]{2,1,0:T(8,128)}) custom-call(f32[15,120,128]{2,1,0:T(8,128)} %bitcast.7, f32[120,128]{1,0:T(8,128)} %bitcast.9, f32[7,120,128]{2,1,0:T(8,128)} %bitcast.8, f32[7,120,120]{2,1,0:T(8,128)} %cpl.1), custom_call_target="tpu_custom_call" | custom-call | tf_op jit(solution)/shard_map/pallas_call | solution.py:370
  76.5 2.5 %add_bitcast_fusion = f32[15,1,120,128]{3,2,1,0:T(8,128)} fusion(f32[15,120,128]{2,1,0:T(8,128)} %get-tuple-element.7, f32[15,120,128]{2,1,0:T(8,128)} %get-tuple-element.8), kind=kLoop, calls=%fused_computation | loop fusion | flops 230400 | bytes 2764800 | tf_op jit(solution)/shard_map/reshape | solution.py:403

commit v5 on v4

--- a/solution.py
+++ b/solution.py
@@ -21,8 +21,8 @@
 OUT2 = 2 * MP
 PR = NY + 16
 KD = 3 * NX * MP
-BACK = 3
-LATE = 6
+BACK = 4
+LATE = 8
 SEAM = 0
 AHEAD = 3
 LAG = 2

time: 79.8 us -> 80.1 us (level)
  the two profiles are of different devices: /device:TPU:1 before, /device:TPU:36 now
where the time goes in v5:
time: 80.1 us; the launch traced here: 80 us
  Pallas kernels  77.5 us (97%)
  other arithmetic  2.47 us (3%)
    pallas_call x1, Pallas kernels, local(): pl.pallas_call(kernel, out_shape=(plane, plane), in_specs=[hbm] * 4, out_...  77.5 us
    reshape x1, other arithmetic, local(): return (own + other).reshape(MD, 1, NY, NZ)  2.47 us

profile of v5, /device:TPU:36, one launch (start us, length us, event | category | flops | bytes accessed | tf_op | source)
XLA Modules:
  0.0 80.0 jit_solution(5155475397174621084)
XLA Ops:
  0.0 77.5 %shard_map.46 = (f32[15,120,128]{2,1,0:T(8,128)}, f32[15,120,128]{2,1,0:T(8,128)}) custom-call(f32[15,120,128]{2,1,0:T(8,128)} %bitcast.7, f32[120,128]{1,0:T(8,128)} %bitcast.9, f32[7,120,128]{2,1,0:T(8,128)} %bitcast.8, f32[7,120,120]{2,1,0:T(8,128)} %cpl.1), custom_call_target="tpu_custom_call" | custom-call | tf_op jit(solution)/shard_map/pallas_call | solution.py:370
  77.5 2.5 %add_bitcast_fusion = f32[15,1,120,128]{3,2,1,0:T(8,128)} fusion(f32[15,120,128]{2,1,0:T(8,128)} %get-tuple-element.7, f32[15,120,128]{2,1,0:T(8,128)} %get-tuple-element.8), kind=kLoop, calls=%fused_computation | loop fusion | flops 230400 | bytes 2764800 | tf_op jit(solution)/shard_map/reshape | solution.py:403
